TPU v7x, 256 devices: a whole 4x4x8 slice. The times are simulated.
256 devices in a mesh: row: 16 (over z, core), col: 16 (over y, x).
Axes of the slice: x: 4, y: 4, z: 8, core: 2. Of those that a mesh axis runs over, the one named last changes fastest.
Arguments:
- sigma_anc: float32 [48, 48, 128, 128], P('row', 'col'), as said below
- factor: float32 [16, 256, 128, 128], P('row', 'col'), may hold values from -1.25 to 1.25
- diag_inv: float32 [256, 128, 128], P('col'), as said below
- struct: int32 [256, 16], P('col'), may hold values from 0 to 47, all different within a row
Outputs:
- z_off: float32 [256, 48, 128, 128], P('col', 'row')
- z_diag: float32 [256, 128, 128], P(('col', 'row'))
Inputs may be any that keep to these rules, and one draw needn't show every extreme that they name: Each row of struct names 16 different ancestor blocks, and every ancestor block is named by some row. sigma_anc is symmetric: block [b, a] is the transpose of block [a, b]. Each diag_inv[k] is lower triangular with a positive diagonal.
All inputs are finite; a program needn't handle non-finite values.
Results may differ from a plain program's by a relative error of at most 0.0003.
Values sent between devices are 32-bit elements; how exact they have to be, the bound alone decides.
A program may use at most 128 MiB of HBM per device.

v0:
```python
import jax
import jax.numpy as jnp
from jax import lax
from jax.sharding import PartitionSpec as P

highest = lax.Precision.HIGHEST


def select_blocks(sigma_rows, slot_ids):
    return jnp.take(sigma_rows, slot_ids, axis=1)


def body(sigma_anc, factor, diag_inv, struct):
    row_count = sigma_anc.shape[0]
    node_count = diag_inv.shape[0]
    width = diag_inv.shape[1]
    row_index = lax.axis_index("row")
    own_rows = row_index * row_count + jnp.arange(row_count, dtype=jnp.int32)
    sigma_rows = lax.all_gather(sigma_anc, "col", axis=1, tiled=True)
    u_local = jnp.einsum("skij,kjl->skil", factor, diag_inv, precision=highest)
    empty = jnp.zeros((node_count, row_count, width, width), jnp.float32)

    def one_slot(running, element):
        u_slot, id_slot = element
        y_sum, u_rows = running
        picked = select_blocks(sigma_rows, id_slot)
        y_sum = y_sum + jnp.einsum("akij,kjl->kail", picked, u_slot, precision=highest)
        match = (id_slot[:, None] == own_rows[None, :]).astype(jnp.float32)
        u_rows = u_rows + match[:, :, None, None] * u_slot[:, None, :, :]
        return ((y_sum, u_rows), None)

    result, unused_out = lax.scan(
        one_slot,
        (empty, empty),
        (lax.all_gather(u_local, "row", axis=0, tiled=True), jnp.transpose(struct)),
    )
    y_rows, u_rows = result
    member = jnp.any(struct[:, :, None] == own_rows[None, None, :], axis=1)
    z_off = jnp.where(member[:, :, None, None], -y_rows, 0.0)
    partial_sum = jnp.einsum("kaij,kail->kjl", u_rows, y_rows, precision=highest)
    share_count = node_count // lax.axis_size("row")
    start_node = row_index * share_count
    inverse_share = lax.dynamic_slice_in_dim(diag_inv, start_node, share_count, 0)
    inverse_part = jnp.einsum("kij,kil->kjl", inverse_share, inverse_share, precision=highest)
    summed = lax.psum(partial_sum, "row")
    mine = lax.dynamic_slice_in_dim(summed, start_node, share_count, 0)
    return (z_off, inverse_part + mine)


def solution(mesh):
    in_specs = (
        P("row", "col", None, None),
        P("row", "col", None, None),
        P("col", None, None),
        P("col", None),
    )
    out_specs = (P("col", "row", None, None), P(("col", "row"), None, None))
    return jax.shard_map(body, mesh=mesh, in_specs=in_specs, out_specs=out_specs, check_vma=False)
```

profile of v0, /device:TPU:1, one launch (start us, length us, event | category | flops | bytes accessed | tf_op | source)
XLA Modules:
  0.0 607.2 jit_solution(9201970120801829042)
XLA Ops:
  13.0 82.0 %all-gather.3.cloned.1.call-done = f32[3,48,128,128]{3,2,1,0:T(8,128)} async-done(((f32[3,3,128,128]{3,2,1,0:T(8,128)}), f32[3,48,128,128]{3,2,1,0:T(8,128)}) %all-gather.3.cloned.1.call-update) | async-done | bytes 9437200 | tf_op jit(solution)/shard_map/all_gather | solution.py:19
  95.0 97.4 %all-gather.5.cloned.1.call-done = f32[16,16,128,128]{3,2,1,0:T(8,128)} async-done(((f32[1,16,128,128]{3,2,1,0:T(8,128)}), f32[16,16,128,128]{3,2,1,0:T(8,128)}) %all-gather.5.cloned.1.call-update) | async-done | bytes 16777232 | tf_op jit(solution)/shard_map/all_gather | solution.py:35
  192.4 287.7 %while.13 = (s32[]{:T(128)}, f32[16,3,128,128]{3,2,1,0:T(8,128)}, f32[16,3,128,128]{3,2,1,0:T(8,128)}, s32[16,16]{1,0:T(8,128)S(1)}, f32[3,48,128,128]{3,2,1,0:T...) while((s32[]{:T(128)}, f32[16,3,128,128]{3,2,1,0:T(8,128)}, ...), condition=%wide.region_2.3_spmd.clone, body=%wide.region_1.2_spmd.clone.sunk | while | flops 1212679424 | bytes 26220016 | solution.py:32
  192.5 6.1 gather_fusion
  198.5 6.2 %select_add_fusion.4 = f32[16,3,128,128]{3,2,1,0:T(8,128)} fusion(f32[16,3,128,128]{3,2,1,0:T(8,128)} %get-tuple-element.149, f32[16,3,128,128]{3,2,1,0:T(8,128)} %gather_fusion, pred[16]{0:T(512)(128)(4,1)S(1)} %get-tuple-element.137, pred[]{:T(512)S(6)} %compare.3, f32[16,16,128,128]{3,2,1,0:T(8,128)} %get-tuple-element.162, s32[]{:T(128)} %get-tuple-element.148), kind=kOutput, calls=%fused_computation.5.clone.1 | convolution fusion | flops 1210318848 | bytes 10486289 | tf_op jit(solution)/shard_map/while/body/eval_jaxpr/akij,kjl->kail/dot_general | solution.py:27
  208.2 6.1 gather_fusion
  214.3 6.7 %select_add_fusion.4 = f32[16,3,128,128]{3,2,1,0:T(8,128)} fusion(f32[16,3,128,128]{3,2,1,0:T(8,128)} %get-tuple-element.149, f32[16,3,128,128]{3,2,1,0:T(8,128)} %gather_fusion, pred[16]{0:T(512)(128)(4,1)S(1)} %get-tuple-element.137, pred[]{:T(512)S(6)} %compare.3, f32[16,16,128,128]{3,2,1,0:T(8,128)} %get-tuple-element.162, s32[]{:T(128)} %get-tuple-element.148), kind=kOutput, calls=%fused_computation.5.clone.1 | convolution fusion | flops 1210318848 | bytes 10486289 | tf_op jit(solution)/shard_map/while/body/eval_jaxpr/akij,kjl->kail/dot_general | solution.py:27
  222.4 4.0 select_add_fusion.5
  226.4 6.1 gather_fusion
  232.4 6.7 %select_add_fusion.4 = f32[16,3,128,128]{3,2,1,0:T(8,128)} fusion(f32[16,3,128,128]{3,2,1,0:T(8,128)} %get-tuple-element.149, f32[16,3,128,128]{3,2,1,0:T(8,128)} %gather_fusion, pred[16]{0:T(512)(128)(4,1)S(1)} %get-tuple-element.137, pred[]{:T(512)S(6)} %compare.3, f32[16,16,128,128]{3,2,1,0:T(8,128)} %get-tuple-element.162, s32[]{:T(128)} %get-tuple-element.148), kind=kOutput, calls=%fused_computation.5.clone.1 | convolution fusion | flops 1210318848 | bytes 10486289 | tf_op jit(solution)/shard_map/while/body/eval_jaxpr/akij,kjl->kail/dot_general | solution.py:27
  240.5 4.0 select_add_fusion.5
  244.5 6.1 gather_fusion
  250.6 6.7 %select_add_fusion.4 = f32[16,3,128,128]{3,2,1,0:T(8,128)} fusion(f32[16,3,128,128]{3,2,1,0:T(8,128)} %get-tuple-element.149, f32[16,3,128,128]{3,2,1,0:T(8,128)} %gather_fusion, pred[16]{0:T(512)(128)(4,1)S(1)} %get-tuple-element.137, pred[]{:T(512)S(6)} %compare.3, f32[16,16,128,128]{3,2,1,0:T(8,128)} %get-tuple-element.162, s32[]{:T(128)} %get-tuple-element.148), kind=kOutput, calls=%fused_computation.5.clone.1 | convolution fusion | flops 1210318848 | bytes 10486289 | tf_op jit(solution)/shard_map/while/body/eval_jaxpr/akij,kjl->kail/dot_general | solution.py:27
  258.6 4.0 select_add_fusion.5
  262.6 6.1 gather_fusion
  268.7 6.7 %select_add_fusion.4 = f32[16,3,128,128]{3,2,1,0:T(8,128)} fusion(f32[16,3,128,128]{3,2,1,0:T(8,128)} %get-tuple-element.149, f32[16,3,128,128]{3,2,1,0:T(8,128)} %gather_fusion, pred[16]{0:T(512)(128)(4,1)S(1)} %get-tuple-element.137, pred[]{:T(512)S(6)} %compare.3, f32[16,16,128,128]{3,2,1,0:T(8,128)} %get-tuple-element.162, s32[]{:T(128)} %get-tuple-element.148), kind=kOutput, calls=%fused_computation.5.clone.1 | convolution fusion | flops 1210318848 | bytes 10486289 | tf_op jit(solution)/shard_map/while/body/eval_jaxpr/akij,kjl->kail/dot_general | solution.py:27
  276.8 4.0 select_add_fusion.5
  280.7 6.1 gather_fusion
  286.8 6.7 %select_add_fusion.4 = f32[16,3,128,128]{3,2,1,0:T(8,128)} fusion(f32[16,3,128,128]{3,2,1,0:T(8,128)} %get-tuple-element.149, f32[16,3,128,128]{3,2,1,0:T(8,128)} %gather_fusion, pred[16]{0:T(512)(128)(4,1)S(1)} %get-tuple-element.137, pred[]{:T(512)S(6)} %compare.3, f32[16,16,128,128]{3,2,1,0:T(8,128)} %get-tuple-element.162, s32[]{:T(128)} %get-tuple-element.148), kind=kOutput, calls=%fused_computation.5.clone.1 | convolution fusion | flops 1210318848 | bytes 10486289 | tf_op jit(solution)/shard_map/while/body/eval_jaxpr/akij,kjl->kail/dot_general | solution.py:27
  294.9 4.0 select_add_fusion.5
  298.9 6.1 gather_fusion
  305.0 6.7 %select_add_fusion.4 = f32[16,3,128,128]{3,2,1,0:T(8,128)} fusion(f32[16,3,128,128]{3,2,1,0:T(8,128)} %get-tuple-element.149, f32[16,3,128,128]{3,2,1,0:T(8,128)} %gather_fusion, pred[16]{0:T(512)(128)(4,1)S(1)} %get-tuple-element.137, pred[]{:T(512)S(6)} %compare.3, f32[16,16,128,128]{3,2,1,0:T(8,128)} %get-tuple-element.162, s32[]{:T(128)} %get-tuple-element.148), kind=kOutput, calls=%fused_computation.5.clone.1 | convolution fusion | flops 1210318848 | bytes 10486289 | tf_op jit(solution)/shard_map/while/body/eval_jaxpr/akij,kjl->kail/dot_general | solution.py:27
  313.0 4.0 select_add_fusion.5
  317.0 6.1 gather_fusion
  323.1 6.7 %select_add_fusion.4 = f32[16,3,128,128]{3,2,1,0:T(8,128)} fusion(f32[16,3,128,128]{3,2,1,0:T(8,128)} %get-tuple-element.149, f32[16,3,128,128]{3,2,1,0:T(8,128)} %gather_fusion, pred[16]{0:T(512)(128)(4,1)S(1)} %get-tuple-element.137, pred[]{:T(512)S(6)} %compare.3, f32[16,16,128,128]{3,2,1,0:T(8,128)} %get-tuple-element.162, s32[]{:T(128)} %get-tuple-element.148), kind=kOutput, calls=%fused_computation.5.clone.1 | convolution fusion | flops 1210318848 | bytes 10486289 | tf_op jit(solution)/shard_map/while/body/eval_jaxpr/akij,kjl->kail/dot_general | solution.py:27
  331.2 4.0 select_add_fusion.5
  335.1 6.1 gather_fusion
  341.2 6.7 %select_add_fusion.4 = f32[16,3,128,128]{3,2,1,0:T(8,128)} fusion(f32[16,3,128,128]{3,2,1,0:T(8,128)} %get-tuple-element.149, f32[16,3,128,128]{3,2,1,0:T(8,128)} %gather_fusion, pred[16]{0:T(512)(128)(4,1)S(1)} %get-tuple-element.137, pred[]{:T(512)S(6)} %compare.3, f32[16,16,128,128]{3,2,1,0:T(8,128)} %get-tuple-element.162, s32[]{:T(128)} %get-tuple-element.148), kind=kOutput, calls=%fused_computation.5.clone.1 | convolution fusion | flops 1210318848 | bytes 10486289 | tf_op jit(solution)/shard_map/while/body/eval_jaxpr/akij,kjl->kail/dot_general | solution.py:27
  349.3 4.0 select_add_fusion.5
  353.3 6.1 gather_fusion
  359.4 6.7 %select_add_fusion.4 = f32[16,3,128,128]{3,2,1,0:T(8,128)} fusion(f32[16,3,128,128]{3,2,1,0:T(8,128)} %get-tuple-element.149, f32[16,3,128,128]{3,2,1,0:T(8,128)} %gather_fusion, pred[16]{0:T(512)(128)(4,1)S(1)} %get-tuple-element.137, pred[]{:T(512)S(6)} %compare.3, f32[16,16,128,128]{3,2,1,0:T(8,128)} %get-tuple-element.162, s32[]{:T(128)} %get-tuple-element.148), kind=kOutput, calls=%fused_computation.5.clone.1 | convolution fusion | flops 1210318848 | bytes 10486289 | tf_op jit(solution)/shard_map/while/body/eval_jaxpr/akij,kjl->kail/dot_general | solution.py:27
  367.4 4.0 select_add_fusion.5
  371.4 6.1 gather_fusion
  377.5 6.7 %select_add_fusion.4 = f32[16,3,128,128]{3,2,1,0:T(8,128)} fusion(f32[16,3,128,128]{3,2,1,0:T(8,128)} %get-tuple-element.149, f32[16,3,128,128]{3,2,1,0:T(8,128)} %gather_fusion, pred[16]{0:T(512)(128)(4,1)S(1)} %get-tuple-element.137, pred[]{:T(512)S(6)} %compare.3, f32[16,16,128,128]{3,2,1,0:T(8,128)} %get-tuple-element.162, s32[]{:T(128)} %get-tuple-element.148), kind=kOutput, calls=%fused_computation.5.clone.1 | convolution fusion | flops 1210318848 | bytes 10486289 | tf_op jit(solution)/shard_map/while/body/eval_jaxpr/akij,kjl->kail/dot_general | solution.py:27
  385.6 4.0 select_add_fusion.5
  389.5 6.1 gather_fusion
  395.6 6.7 %select_add_fusion.4 = f32[16,3,128,128]{3,2,1,0:T(8,128)} fusion(f32[16,3,128,128]{3,2,1,0:T(8,128)} %get-tuple-element.149, f32[16,3,128,128]{3,2,1,0:T(8,128)} %gather_fusion, pred[16]{0:T(512)(128)(4,1)S(1)} %get-tuple-element.137, pred[]{:T(512)S(6)} %compare.3, f32[16,16,128,128]{3,2,1,0:T(8,128)} %get-tuple-element.162, s32[]{:T(128)} %get-tuple-element.148), kind=kOutput, calls=%fused_computation.5.clone.1 | convolution fusion | flops 1210318848 | bytes 10486289 | tf_op jit(solution)/shard_map/while/body/eval_jaxpr/akij,kjl->kail/dot_general | solution.py:27
  403.7 4.0 select_add_fusion.5
  407.7 6.1 gather_fusion
  413.8 6.7 %select_add_fusion.4 = f32[16,3,128,128]{3,2,1,0:T(8,128)} fusion(f32[16,3,128,128]{3,2,1,0:T(8,128)} %get-tuple-element.149, f32[16,3,128,128]{3,2,1,0:T(8,128)} %gather_fusion, pred[16]{0:T(512)(128)(4,1)S(1)} %get-tuple-element.137, pred[]{:T(512)S(6)} %compare.3, f32[16,16,128,128]{3,2,1,0:T(8,128)} %get-tuple-element.162, s32[]{:T(128)} %get-tuple-element.148), kind=kOutput, calls=%fused_computation.5.clone.1 | convolution fusion | flops 1210318848 | bytes 10486289 | tf_op jit(solution)/shard_map/while/body/eval_jaxpr/akij,kjl->kail/dot_general | solution.py:27
  425.8 6.1 gather_fusion
  431.9 6.7 %select_add_fusion.4 = f32[16,3,128,128]{3,2,1,0:T(8,128)} fusion(f32[16,3,128,128]{3,2,1,0:T(8,128)} %get-tuple-element.149, f32[16,3,128,128]{3,2,1,0:T(8,128)} %gather_fusion, pred[16]{0:T(512)(128)(4,1)S(1)} %get-tuple-element.137, pred[]{:T(512)S(6)} %compare.3, f32[16,16,128,128]{3,2,1,0:T(8,128)} %get-tuple-element.162, s32[]{:T(128)} %get-tuple-element.148), kind=kOutput, calls=%fused_computation.5.clone.1 | convolution fusion | flops 1210318848 | bytes 10486289 | tf_op jit(solution)/shard_map/while/body/eval_jaxpr/akij,kjl->kail/dot_general | solution.py:27
  443.9 6.1 gather_fusion
  450.0 6.7 %select_add_fusion.4 = f32[16,3,128,128]{3,2,1,0:T(8,128)} fusion(f32[16,3,128,128]{3,2,1,0:T(8,128)} %get-tuple-element.149, f32[16,3,128,128]{3,2,1,0:T(8,128)} %gather_fusion, pred[16]{0:T(512)(128)(4,1)S(1)} %get-tuple-element.137, pred[]{:T(512)S(6)} %compare.3, f32[16,16,128,128]{3,2,1,0:T(8,128)} %get-tuple-element.162, s32[]{:T(128)} %get-tuple-element.148), kind=kOutput, calls=%fused_computation.5.clone.1 | convolution fusion | flops 1210318848 | bytes 10486289 | tf_op jit(solution)/shard_map/while/body/eval_jaxpr/akij,kjl->kail/dot_general | solution.py:27
  462.1 6.1 gather_fusion
  468.2 6.7 %select_add_fusion.4 = f32[16,3,128,128]{3,2,1,0:T(8,128)} fusion(f32[16,3,128,128]{3,2,1,0:T(8,128)} %get-tuple-element.149, f32[16,3,128,128]{3,2,1,0:T(8,128)} %gather_fusion, pred[16]{0:T(512)(128)(4,1)S(1)} %get-tuple-element.137, pred[]{:T(512)S(6)} %compare.3, f32[16,16,128,128]{3,2,1,0:T(8,128)} %get-tuple-element.162, s32[]{:T(128)} %get-tuple-element.148), kind=kOutput, calls=%fused_computation.5.clone.1 | convolution fusion | flops 1210318848 | bytes 10486289 | tf_op jit(solution)/shard_map/while/body/eval_jaxpr/akij,kjl->kail/dot_general | solution.py:27
  480.2 9.0 %convolution_bitcast_fusion = f32[16,128,128]{2,1,0:T(8,128)} fusion(f32[16,3,128,128]{3,2,1,0:T(8,128)} %get-tuple-element.41, f32[16,3,128,128]{3,2,1,0:T(8,128)} %get-tuple-element.40), kind=kOutput, calls=%fused_computation.24 | convolution fusion | flops 1207959552 | bytes 7340032 | tf_op jit(solution)/shard_map/kaij,kail->kjl/dot_general | solution.py:40
  493.4 105.4 %all-reduce.2.cloned.1.call-done = f32[16,128,128]{2,1,0:T(8,128)} async-done(((f32[16,128,128]{2,1,0:T(8,128)}), f32[16,128,128]{2,1,0:T(8,128)}) %all-reduce.2.cloned.1.call-update) | async-done | bytes 1048592 | tf_op jit(solution)/shard_map/psum | solution.py:45
  (121 shorter events, 52.1 us)
Async XLA Ops:
  7.2 1.2 copy-start
  7.2 87.8 %all-gather.3.cloned.1.call-start = ((), (), s32[]{:S(2)}) async-start(), calls=%async_computation | async-start | bytes 10027008 | tf_op jit(solution)/shard_map/all_gather | solution.py:19
  7.9 5.0 copy-start.1
  7.9 184.5 %all-gather.5.cloned.1.call-start = ((), (), s32[]{:S(2)}) async-start(), calls=%async_computation.1 | async-start | bytes 17825792 | tf_op jit(solution)/shard_map/all_gather | solution.py:35
  12.8 586.0 %all-reduce.2.cloned.1.call-start = ((), (), s32[]{:S(2)}) async-start(), calls=%async_computation.2 | async-start | bytes 2097152 | tf_op jit(solution)/shard_map/psum | solution.py:45
Sparse Core Ops, SparseCore 0:
  10.4 84.5 all-gather.2
  96.8 95.5 all-gather.4
  489.3 109.5 all-reduce.1
where the time goes:
time: 609 us; the launch traced here: 607 us
  waiting for transfers between devices  286 us (47%)
  local copies, waits for them, and re-layouts  120 us (20%)
  matrix products  120 us (20%)
  other arithmetic  67.3 us (11%)
  between operations  13.8 us (2%)
    dot_general x16, matrix products, one_slot(): jnp.einsum('akij,kjl->kail', picked, u_slot, precision=highest)  106 us
    psum x1, waiting for transfers between devices, body(): summed = lax.psum(partial_sum, 'row')  105 us
    all_gather x1, waiting for transfers between devices, body(): lax.all_gather(u_local, 'row', axis=0, tiled=True)  97.4 us
    gather x16, local copies, waits for them, and re-layouts, select_blocks(): return jnp.take(sigma_rows, slot_ids, axis=1)  97.1 us
    all_gather x1, waiting for transfers between devices, body(): sigma_rows = lax.all_gather(sigma_anc, 'col', axis=1, tiled=True)  82 us
    add x16, other arithmetic, one_slot(): u_rows = u_rows + match[:, :, None, None] * u_slot[:, None, :, :]  61.5 us
    squeeze x16, local copies, waits for them, and re-layouts, body(): lax.scan(one_slot, (empty, empty), (lax.all_gather(u_local, 'row', axis=0...  20.7 us
  transfers between devices with their start and end apart: 3, of which 3 were waited for; matrix products, arithmetic and copies ran while one was open for 1% of the time, Pallas kernels for 0%

commit v1 on v0

--- a/solution.py
+++ b/solution.py
@@ -4,6 +4,24 @@
 from jax.sharding import PartitionSpec as P
 
 highest = lax.Precision.HIGHEST
+
+
+def gather_around(shard, axis, dim):
+    ways, here, step = (lax.axis_size(axis), lax.axis_index(axis), shard.shape[dim])
+    shape = [n * ways if d == dim else n for d, n in enumerate(shard.shape)]
+    full = lax.dynamic_update_slice_in_dim(
+        jnp.zeros(shape, shard.dtype), shard, here * step, axis=dim
+    )
+    going_up = going_down = shard
+    for far in range(1, ways // 2 + 1):
+        going_up = lax.ppermute(going_up, axis, [(d, (d + 1) % ways) for d in range(ways)])
+        full = lax.dynamic_update_slice_in_dim(full, going_up, (here - far) % ways * step, axis=dim)
+        if 2 * far < ways:
+            going_down = lax.ppermute(going_down, axis, [(d, (d - 1) % ways) for d in range(ways)])
+            full = lax.dynamic_update_slice_in_dim(
+                full, going_down, (here + far) % ways * step, axis=dim
+            )
+    return full
 
 
 def select_blocks(sigma_rows, slot_ids):
@@ -16,7 +34,7 @@
     width = diag_inv.shape[1]
     row_index = lax.axis_index("row")
     own_rows = row_index * row_count + jnp.arange(row_count, dtype=jnp.int32)
-    sigma_rows = lax.all_gather(sigma_anc, "col", axis=1, tiled=True)
+    sigma_rows = gather_around(sigma_anc, "col", 1)
     u_local = jnp.einsum("skij,kjl->skil", factor, diag_inv, precision=highest)
     empty = jnp.zeros((node_count, row_count, width, width), jnp.float32)
 

time: 609 us -> 560 us (0.920)
  waiting for transfers between devices: 286 us -> 176 us
  starting transfers between devices: 0.12 us -> 35.3 us
  local copies, waits for them, and re-layouts: 120 us -> 143 us
    all_gather x1, waiting for transfers between devices: 97.4 us -> 0.01 us  [body(): lax.all_gather(u_local, 'row', axis=0, tiled=True)]
    all_gather x1 -> x0, waiting for transfers between devices: 82 us -> none  [body(): sigma_rows = lax.all_gather(sigma_anc, 'col', axis=1, tiled=True)]
    ppermute x0 -> x15, waiting for transfers between devices: none -> 55.2 us  [the longest x8 51.2 us: gather_around(): lax.ppermute(going_up, axis, [(d, (d + 1) % ways) for d in range(ways)])]
    ppermute x0 -> x15, starting transfers between devices: none -> 35.2 us  [the longest x7 33.1 us: gather_around(): lax.ppermute(going_down, axis, [(d, (d - 1) % ways) for d in range(ways)])]
    dynamic_update_slice x0 -> x16, local copies, waits for them, and re-layouts: none -> 17.2 us  [the longest x8 9.08 us: gather_around(): lax.dynamic_update_slice_in_dim(full, going_up, (here - far) % ways * ste...]
    psum x1, waiting for transfers between devices: 105 us -> 120 us  [body(): summed = lax.psum(partial_sum, 'row')]
  transfers between devices with their start and end apart: 3 -> 17, of which waited for: 3 -> 9; matrix products, arithmetic and copies ran while one was open for 1% -> 5% of each run, Pallas kernels for 0% -> 0%
where the time goes in v1:
time: 560 us; the launch traced here: 557 us
  waiting for transfers between devices  176 us (31%)
  local copies, waits for them, and re-layouts  143 us (26%)
  matrix products  120 us (21%)
  other arithmetic  68.2 us (12%)
  starting transfers between devices  35.3 us (6%)
  between operations  14.2 us (3%)
    psum x1, waiting for transfers between devices, body(): summed = lax.psum(partial_sum, 'row')  120 us
    dot_general x16, matrix products, one_slot(): jnp.einsum('akij,kjl->kail', picked, u_slot, precision=highest)  107 us
    gather x16, local copies, waits for them, and re-layouts, select_blocks(): return jnp.take(sigma_rows, slot_ids, axis=1)  97.3 us
    add x16, other arithmetic, one_slot(): u_rows = u_rows + match[:, :, None, None] * u_slot[:, None, :, :]  62.4 us
    ppermute x8, waiting for transfers between devices, gather_around(): lax.ppermute(going_up, axis, [(d, (d + 1) % ways) for d in range(ways)])  51.2 us
    ppermute x7, starting transfers between devices, gather_around(): lax.ppermute(going_down, axis, [(d, (d - 1) % ways) for d in range(ways)])  33.1 us
    squeeze x16, local copies, waits for them, and re-layouts, body(): lax.scan(one_slot, (empty, empty), (lax.all_gather(u_local, 'row', axis=0...  20.7 us
  transfers between devices with their start and end apart: 17, of which 9 were waited for; matrix products, arithmetic and copies ran while one was open for 5% of the time, Pallas kernels for 0%

profile of v1, /device:TPU:1, one launch (start us, length us, event | category | flops | bytes accessed | tf_op | source)
XLA Modules:
  0.0 557.4 jit_solution(12089556227682561473)
XLA Ops:
  18.8 11.2 %collective-permute-done = f32[3,3,128,128]{3,2,1,0:T(8,128)S(1)} collective-permute-done((f32[3,3,128,128]{3,2,1,0:T(8,128)}, f32[3,3,128,128]{3,2,1,0:T(8,128)S(1)}, u32[]{:S(2)}, u32[]{:S(2)}) %collective-permute-start) | collective-permute-done | bytes 589856 | tf_op jit(solution)/shard_map/ppermute | solution.py:17
  30.0 4.8 collective-permute-start.3
  34.8 10.2 %collective-permute-done.2 = f32[3,3,128,128]{3,2,1,0:T(8,128)S(1)} collective-permute-done((f32[3,3,128,128]{3,2,1,0:T(8,128)S(1)}, f32[3,3,128,128]{3,2,1,0:T(8,128)S(1)}, u32[]{:S(2)}, u32[]{:S(2)}) %collective-permute-start.2) | collective-permute-done | bytes 589856 | tf_op jit(solution)/shard_map/ppermute | solution.py:17
  45.0 4.8 collective-permute-start.5
  49.9 9.2 %collective-permute-done.4 = f32[3,3,128,128]{3,2,1,0:T(8,128)S(1)} collective-permute-done((f32[3,3,128,128]{3,2,1,0:T(8,128)S(1)}, f32[3,3,128,128]{3,2,1,0:T(8,128)S(1)}, u32[]{:S(2)}, u32[]{:S(2)}) %collective-permute-start.4) | collective-permute-done | bytes 589856 | tf_op jit(solution)/shard_map/ppermute | solution.py:17
  59.0 4.8 collective-permute-start.7
  63.8 8.4 %collective-permute-done.6 = f32[3,3,128,128]{3,2,1,0:T(8,128)} collective-permute-done((f32[3,3,128,128]{3,2,1,0:T(8,128)S(1)}, f32[3,3,128,128]{3,2,1,0:T(8,128)}, u32[]{:S(2)}, u32[]{:S(2)}) %collective-permute-start.6) | collective-permute-done | bytes 589856 | tf_op jit(solution)/shard_map/ppermute | solution.py:17
  72.3 4.9 collective-permute-start.9
  77.9 6.7 %collective-permute-done.8 = f32[3,3,128,128]{3,2,1,0:T(8,128)} collective-permute-done((f32[3,3,128,128]{3,2,1,0:T(8,128)}, f32[3,3,128,128]{3,2,1,0:T(8,128)}, u32[]{:S(2)}, u32[]{:S(2)}) %collective-permute-start.8) | collective-permute-done | bytes 589856 | tf_op jit(solution)/shard_map/ppermute | solution.py:17
  84.6 4.8 broadcast_in_dim.35
  92.9 4.8 collective-permute-start.11
  104.6 5.2 collective-permute-start.13
  119.9 5.5 collective-permute-done.14
  126.3 288.9 %while.13 = (s32[]{:T(128)}, f32[16,3,128,128]{3,2,1,0:T(8,128)}, f32[16,3,128,128]{3,2,1,0:T(8,128)}, s32[16,16]{1,0:T(8,128)S(1)}, f32[3,48,128,128]{3,2,1,0:T...) while((s32[]{:T(128)}, f32[16,3,128,128]{3,2,1,0:T(8,128)}, ...), condition=%wide.region_2.3_spmd.clone, body=%wide.region_1.2_spmd.clone.sunk | while | flops 1212679424 | bytes 26220016 | solution.py:50
  126.3 6.1 %gather_fusion = f32[16,3,128,128]{3,2,1,0:T(8,128)} fusion(f32[3,48,128,128]{3,2,1,0:T(8,128)} %get-tuple-element.161, s32[1024]{0:T(1024)S(1)} %pad_clamp_fusion.2), kind=kCustom, calls=%fused_computation.clone.clone.1 | custom fusion | bytes 6291520 | tf_op jit(solution)/shard_map/while/body/eval_jaxpr/jit(_take)/gather | solution.py:28
  132.4 6.2 %select_add_fusion.4 = f32[16,3,128,128]{3,2,1,0:T(8,128)} fusion(f32[16,3,128,128]{3,2,1,0:T(8,128)} %get-tuple-element.149, f32[16,3,128,128]{3,2,1,0:T(8,128)} %gather_fusion, pred[16]{0:T(512)(128)(4,1)S(1)} %get-tuple-element.137, pred[]{:T(512)S(6)} %compare.18, f32[16,16,128,128]{3,2,1,0:T(8,128)} %get-tuple-element.162, s32[]{:T(128)} %get-tuple-element.148), kind=kOutput, calls=%fused_computation.5.clone.1 | convolution fusion | flops 1210318848 | bytes 10486289 | tf_op jit(solution)/shard_map/while/body/eval_jaxpr/akij,kjl->kail/dot_general | solution.py:45
  142.1 6.1 %gather_fusion = f32[16,3,128,128]{3,2,1,0:T(8,128)} fusion(f32[3,48,128,128]{3,2,1,0:T(8,128)} %get-tuple-element.161, s32[1024]{0:T(1024)S(1)} %pad_clamp_fusion.2), kind=kCustom, calls=%fused_computation.clone.clone.1 | custom fusion | bytes 6291520 | tf_op jit(solution)/shard_map/while/body/eval_jaxpr/jit(_take)/gather | solution.py:28
  148.2 6.7 %select_add_fusion.4 = f32[16,3,128,128]{3,2,1,0:T(8,128)} fusion(f32[16,3,128,128]{3,2,1,0:T(8,128)} %get-tuple-element.149, f32[16,3,128,128]{3,2,1,0:T(8,128)} %gather_fusion, pred[16]{0:T(512)(128)(4,1)S(1)} %get-tuple-element.137, pred[]{:T(512)S(6)} %compare.18, f32[16,16,128,128]{3,2,1,0:T(8,128)} %get-tuple-element.162, s32[]{:T(128)} %get-tuple-element.148), kind=kOutput, calls=%fused_computation.5.clone.1 | convolution fusion | flops 1210318848 | bytes 10486289 | tf_op jit(solution)/shard_map/while/body/eval_jaxpr/akij,kjl->kail/dot_general | solution.py:45
  160.3 6.1 %gather_fusion = f32[16,3,128,128]{3,2,1,0:T(8,128)} fusion(f32[3,48,128,128]{3,2,1,0:T(8,128)} %get-tuple-element.161, s32[1024]{0:T(1024)S(1)} %pad_clamp_fusion.2), kind=kCustom, calls=%fused_computation.clone.clone.1 | custom fusion | bytes 6291520 | tf_op jit(solution)/shard_map/while/body/eval_jaxpr/jit(_take)/gather | solution.py:28
  166.4 6.7 %select_add_fusion.4 = f32[16,3,128,128]{3,2,1,0:T(8,128)} fusion(f32[16,3,128,128]{3,2,1,0:T(8,128)} %get-tuple-element.149, f32[16,3,128,128]{3,2,1,0:T(8,128)} %gather_fusion, pred[16]{0:T(512)(128)(4,1)S(1)} %get-tuple-element.137, pred[]{:T(512)S(6)} %compare.18, f32[16,16,128,128]{3,2,1,0:T(8,128)} %get-tuple-element.162, s32[]{:T(128)} %get-tuple-element.148), kind=kOutput, calls=%fused_computation.5.clone.1 | convolution fusion | flops 1210318848 | bytes 10486289 | tf_op jit(solution)/shard_map/while/body/eval_jaxpr/akij,kjl->kail/dot_general | solution.py:45
  178.5 6.1 %gather_fusion = f32[16,3,128,128]{3,2,1,0:T(8,128)} fusion(f32[3,48,128,128]{3,2,1,0:T(8,128)} %get-tuple-element.161, s32[1024]{0:T(1024)S(1)} %pad_clamp_fusion.2), kind=kCustom, calls=%fused_computation.clone.clone.1 | custom fusion | bytes 6291520 | tf_op jit(solution)/shard_map/while/body/eval_jaxpr/jit(_take)/gather | solution.py:28
  184.6 6.7 %select_add_fusion.4 = f32[16,3,128,128]{3,2,1,0:T(8,128)} fusion(f32[16,3,128,128]{3,2,1,0:T(8,128)} %get-tuple-element.149, f32[16,3,128,128]{3,2,1,0:T(8,128)} %gather_fusion, pred[16]{0:T(512)(128)(4,1)S(1)} %get-tuple-element.137, pred[]{:T(512)S(6)} %compare.18, f32[16,16,128,128]{3,2,1,0:T(8,128)} %get-tuple-element.162, s32[]{:T(128)} %get-tuple-element.148), kind=kOutput, calls=%fused_computation.5.clone.1 | convolution fusion | flops 1210318848 | bytes 10486289 | tf_op jit(solution)/shard_map/while/body/eval_jaxpr/akij,kjl->kail/dot_general | solution.py:45
  196.7 6.1 %gather_fusion = f32[16,3,128,128]{3,2,1,0:T(8,128)} fusion(f32[3,48,128,128]{3,2,1,0:T(8,128)} %get-tuple-element.161, s32[1024]{0:T(1024)S(1)} %pad_clamp_fusion.2), kind=kCustom, calls=%fused_computation.clone.clone.1 | custom fusion | bytes 6291520 | tf_op jit(solution)/shard_map/while/body/eval_jaxpr/jit(_take)/gather | solution.py:28
  202.8 6.7 %select_add_fusion.4 = f32[16,3,128,128]{3,2,1,0:T(8,128)} fusion(f32[16,3,128,128]{3,2,1,0:T(8,128)} %get-tuple-element.149, f32[16,3,128,128]{3,2,1,0:T(8,128)} %gather_fusion, pred[16]{0:T(512)(128)(4,1)S(1)} %get-tuple-element.137, pred[]{:T(512)S(6)} %compare.18, f32[16,16,128,128]{3,2,1,0:T(8,128)} %get-tuple-element.162, s32[]{:T(128)} %get-tuple-element.148), kind=kOutput, calls=%fused_computation.5.clone.1 | convolution fusion | flops 1210318848 | bytes 10486289 | tf_op jit(solution)/shard_map/while/body/eval_jaxpr/akij,kjl->kail/dot_general | solution.py:45
  214.9 6.1 %gather_fusion = f32[16,3,128,128]{3,2,1,0:T(8,128)} fusion(f32[3,48,128,128]{3,2,1,0:T(8,128)} %get-tuple-element.161, s32[1024]{0:T(1024)S(1)} %pad_clamp_fusion.2), kind=kCustom, calls=%fused_computation.clone.clone.1 | custom fusion | bytes 6291520 | tf_op jit(solution)/shard_map/while/body/eval_jaxpr/jit(_take)/gather | solution.py:28
  221.0 6.7 %select_add_fusion.4 = f32[16,3,128,128]{3,2,1,0:T(8,128)} fusion(f32[16,3,128,128]{3,2,1,0:T(8,128)} %get-tuple-element.149, f32[16,3,128,128]{3,2,1,0:T(8,128)} %gather_fusion, pred[16]{0:T(512)(128)(4,1)S(1)} %get-tuple-element.137, pred[]{:T(512)S(6)} %compare.18, f32[16,16,128,128]{3,2,1,0:T(8,128)} %get-tuple-element.162, s32[]{:T(128)} %get-tuple-element.148), kind=kOutput, calls=%fused_computation.5.clone.1 | convolution fusion | flops 1210318848 | bytes 10486289 | tf_op jit(solution)/shard_map/while/body/eval_jaxpr/akij,kjl->kail/dot_general | solution.py:45
  233.1 6.1 %gather_fusion = f32[16,3,128,128]{3,2,1,0:T(8,128)} fusion(f32[3,48,128,128]{3,2,1,0:T(8,128)} %get-tuple-element.161, s32[1024]{0:T(1024)S(1)} %pad_clamp_fusion.2), kind=kCustom, calls=%fused_computation.clone.clone.1 | custom fusion | bytes 6291520 | tf_op jit(solution)/shard_map/while/body/eval_jaxpr/jit(_take)/gather | solution.py:28
  239.2 6.7 %select_add_fusion.4 = f32[16,3,128,128]{3,2,1,0:T(8,128)} fusion(f32[16,3,128,128]{3,2,1,0:T(8,128)} %get-tuple-element.149, f32[16,3,128,128]{3,2,1,0:T(8,128)} %gather_fusion, pred[16]{0:T(512)(128)(4,1)S(1)} %get-tuple-element.137, pred[]{:T(512)S(6)} %compare.18, f32[16,16,128,128]{3,2,1,0:T(8,128)} %get-tuple-element.162, s32[]{:T(128)} %get-tuple-element.148), kind=kOutput, calls=%fused_computation.5.clone.1 | convolution fusion | flops 1210318848 | bytes 10486289 | tf_op jit(solution)/shard_map/while/body/eval_jaxpr/akij,kjl->kail/dot_general | solution.py:45
  251.3 6.1 %gather_fusion = f32[16,3,128,128]{3,2,1,0:T(8,128)} fusion(f32[3,48,128,128]{3,2,1,0:T(8,128)} %get-tuple-element.161, s32[1024]{0:T(1024)S(1)} %pad_clamp_fusion.2), kind=kCustom, calls=%fused_computation.clone.clone.1 | custom fusion | bytes 6291520 | tf_op jit(solution)/shard_map/while/body/eval_jaxpr/jit(_take)/gather | solution.py:28
  257.4 6.7 %select_add_fusion.4 = f32[16,3,128,128]{3,2,1,0:T(8,128)} fusion(f32[16,3,128,128]{3,2,1,0:T(8,128)} %get-tuple-element.149, f32[16,3,128,128]{3,2,1,0:T(8,128)} %gather_fusion, pred[16]{0:T(512)(128)(4,1)S(1)} %get-tuple-element.137, pred[]{:T(512)S(6)} %compare.18, f32[16,16,128,128]{3,2,1,0:T(8,128)} %get-tuple-element.162, s32[]{:T(128)} %get-tuple-element.148), kind=kOutput, calls=%fused_computation.5.clone.1 | convolution fusion | flops 1210318848 | bytes 10486289 | tf_op jit(solution)/shard_map/while/body/eval_jaxpr/akij,kjl->kail/dot_general | solution.py:45
  269.5 6.1 %gather_fusion = f32[16,3,128,128]{3,2,1,0:T(8,128)} fusion(f32[3,48,128,128]{3,2,1,0:T(8,128)} %get-tuple-element.161, s32[1024]{0:T(1024)S(1)} %pad_clamp_fusion.2), kind=kCustom, calls=%fused_computation.clone.clone.1 | custom fusion | bytes 6291520 | tf_op jit(solution)/shard_map/while/body/eval_jaxpr/jit(_take)/gather | solution.py:28
  275.6 6.7 %select_add_fusion.4 = f32[16,3,128,128]{3,2,1,0:T(8,128)} fusion(f32[16,3,128,128]{3,2,1,0:T(8,128)} %get-tuple-element.149, f32[16,3,128,128]{3,2,1,0:T(8,128)} %gather_fusion, pred[16]{0:T(512)(128)(4,1)S(1)} %get-tuple-element.137, pred[]{:T(512)S(6)} %compare.18, f32[16,16,128,128]{3,2,1,0:T(8,128)} %get-tuple-element.162, s32[]{:T(128)} %get-tuple-element.148), kind=kOutput, calls=%fused_computation.5.clone.1 | convolution fusion | flops 1210318848 | bytes 10486289 | tf_op jit(solution)/shard_map/while/body/eval_jaxpr/akij,kjl->kail/dot_general | solution.py:45
  287.7 6.1 %gather_fusion = f32[16,3,128,128]{3,2,1,0:T(8,128)} fusion(f32[3,48,128,128]{3,2,1,0:T(8,128)} %get-tuple-element.161, s32[1024]{0:T(1024)S(1)} %pad_clamp_fusion.2), kind=kCustom, calls=%fused_computation.clone.clone.1 | custom fusion | bytes 6291520 | tf_op jit(solution)/shard_map/while/body/eval_jaxpr/jit(_take)/gather | solution.py:28
  293.8 6.7 %select_add_fusion.4 = f32[16,3,128,128]{3,2,1,0:T(8,128)} fusion(f32[16,3,128,128]{3,2,1,0:T(8,128)} %get-tuple-element.149, f32[16,3,128,128]{3,2,1,0:T(8,128)} %gather_fusion, pred[16]{0:T(512)(128)(4,1)S(1)} %get-tuple-element.137, pred[]{:T(512)S(6)} %compare.18, f32[16,16,128,128]{3,2,1,0:T(8,128)} %get-tuple-element.162, s32[]{:T(128)} %get-tuple-element.148), kind=kOutput, calls=%fused_computation.5.clone.1 | convolution fusion | flops 1210318848 | bytes 10486289 | tf_op jit(solution)/shard_map/while/body/eval_jaxpr/akij,kjl->kail/dot_general | solution.py:45
  305.9 6.1 %gather_fusion = f32[16,3,128,128]{3,2,1,0:T(8,128)} fusion(f32[3,48,128,128]{3,2,1,0:T(8,128)} %get-tuple-element.161, s32[1024]{0:T(1024)S(1)} %pad_clamp_fusion.2), kind=kCustom, calls=%fused_computation.clone.clone.1 | custom fusion | bytes 6291520 | tf_op jit(solution)/shard_map/while/body/eval_jaxpr/jit(_take)/gather | solution.py:28
  312.0 6.7 %select_add_fusion.4 = f32[16,3,128,128]{3,2,1,0:T(8,128)} fusion(f32[16,3,128,128]{3,2,1,0:T(8,128)} %get-tuple-element.149, f32[16,3,128,128]{3,2,1,0:T(8,128)} %gather_fusion, pred[16]{0:T(512)(128)(4,1)S(1)} %get-tuple-element.137, pred[]{:T(512)S(6)} %compare.18, f32[16,16,128,128]{3,2,1,0:T(8,128)} %get-tuple-element.162, s32[]{:T(128)} %get-tuple-element.148), kind=kOutput, calls=%fused_computation.5.clone.1 | convolution fusion | flops 1210318848 | bytes 10486289 | tf_op jit(solution)/shard_map/while/body/eval_jaxpr/akij,kjl->kail/dot_general | solution.py:45
  324.1 6.1 %gather_fusion = f32[16,3,128,128]{3,2,1,0:T(8,128)} fusion(f32[3,48,128,128]{3,2,1,0:T(8,128)} %get-tuple-element.161, s32[1024]{0:T(1024)S(1)} %pad_clamp_fusion.2), kind=kCustom, calls=%fused_computation.clone.clone.1 | custom fusion | bytes 6291520 | tf_op jit(solution)/shard_map/while/body/eval_jaxpr/jit(_take)/gather | solution.py:28
  330.2 6.7 %select_add_fusion.4 = f32[16,3,128,128]{3,2,1,0:T(8,128)} fusion(f32[16,3,128,128]{3,2,1,0:T(8,128)} %get-tuple-element.149, f32[16,3,128,128]{3,2,1,0:T(8,128)} %gather_fusion, pred[16]{0:T(512)(128)(4,1)S(1)} %get-tuple-element.137, pred[]{:T(512)S(6)} %compare.18, f32[16,16,128,128]{3,2,1,0:T(8,128)} %get-tuple-element.162, s32[]{:T(128)} %get-tuple-element.148), kind=kOutput, calls=%fused_computation.5.clone.1 | convolution fusion | flops 1210318848 | bytes 10486289 | tf_op jit(solution)/shard_map/while/body/eval_jaxpr/akij,kjl->kail/dot_general | solution.py:45
  342.3 6.1 %gather_fusion = f32[16,3,128,128]{3,2,1,0:T(8,128)} fusion(f32[3,48,128,128]{3,2,1,0:T(8,128)} %get-tuple-element.161, s32[1024]{0:T(1024)S(1)} %pad_clamp_fusion.2), kind=kCustom, calls=%fused_computation.clone.clone.1 | custom fusion | bytes 6291520 | tf_op jit(solution)/shard_map/while/body/eval_jaxpr/jit(_take)/gather | solution.py:28
  348.4 6.7 %select_add_fusion.4 = f32[16,3,128,128]{3,2,1,0:T(8,128)} fusion(f32[16,3,128,128]{3,2,1,0:T(8,128)} %get-tuple-element.149, f32[16,3,128,128]{3,2,1,0:T(8,128)} %gather_fusion, pred[16]{0:T(512)(128)(4,1)S(1)} %get-tuple-element.137, pred[]{:T(512)S(6)} %compare.18, f32[16,16,128,128]{3,2,1,0:T(8,128)} %get-tuple-element.162, s32[]{:T(128)} %get-tuple-element.148), kind=kOutput, calls=%fused_computation.5.clone.1 | convolution fusion | flops 1210318848 | bytes 10486289 | tf_op jit(solution)/shard_map/while/body/eval_jaxpr/akij,kjl->kail/dot_general | solution.py:45
  360.5 6.1 %gather_fusion = f32[16,3,128,128]{3,2,1,0:T(8,128)} fusion(f32[3,48,128,128]{3,2,1,0:T(8,128)} %get-tuple-element.161, s32[1024]{0:T(1024)S(1)} %pad_clamp_fusion.2), kind=kCustom, calls=%fused_computation.clone.clone.1 | custom fusion | bytes 6291520 | tf_op jit(solution)/shard_map/while/body/eval_jaxpr/jit(_take)/gather | solution.py:28
  366.6 6.7 %select_add_fusion.4 = f32[16,3,128,128]{3,2,1,0:T(8,128)} fusion(f32[16,3,128,128]{3,2,1,0:T(8,128)} %get-tuple-element.149, f32[16,3,128,128]{3,2,1,0:T(8,128)} %gather_fusion, pred[16]{0:T(512)(128)(4,1)S(1)} %get-tuple-element.137, pred[]{:T(512)S(6)} %compare.18, f32[16,16,128,128]{3,2,1,0:T(8,128)} %get-tuple-element.162, s32[]{:T(128)} %get-tuple-element.148), kind=kOutput, calls=%fused_computation.5.clone.1 | convolution fusion | flops 1210318848 | bytes 10486289 | tf_op jit(solution)/shard_map/while/body/eval_jaxpr/akij,kjl->kail/dot_general | solution.py:45
  378.7 6.1 %gather_fusion = f32[16,3,128,128]{3,2,1,0:T(8,128)} fusion(f32[3,48,128,128]{3,2,1,0:T(8,128)} %get-tuple-element.161, s32[1024]{0:T(1024)S(1)} %pad_clamp_fusion.2), kind=kCustom, calls=%fused_computation.clone.clone.1 | custom fusion | bytes 6291520 | tf_op jit(solution)/shard_map/while/body/eval_jaxpr/jit(_take)/gather | solution.py:28
  384.8 6.7 %select_add_fusion.4 = f32[16,3,128,128]{3,2,1,0:T(8,128)} fusion(f32[16,3,128,128]{3,2,1,0:T(8,128)} %get-tuple-element.149, f32[16,3,128,128]{3,2,1,0:T(8,128)} %gather_fusion, pred[16]{0:T(512)(128)(4,1)S(1)} %get-tuple-element.137, pred[]{:T(512)S(6)} %compare.18, f32[16,16,128,128]{3,2,1,0:T(8,128)} %get-tuple-element.162, s32[]{:T(128)} %get-tuple-element.148), kind=kOutput, calls=%fused_computation.5.clone.1 | convolution fusion | flops 1210318848 | bytes 10486289 | tf_op jit(solution)/shard_map/while/body/eval_jaxpr/akij,kjl->kail/dot_general | solution.py:45
  397.0 6.1 %gather_fusion = f32[16,3,128,128]{3,2,1,0:T(8,128)} fusion(f32[3,48,128,128]{3,2,1,0:T(8,128)} %get-tuple-element.161, s32[1024]{0:T(1024)S(1)} %pad_clamp_fusion.2), kind=kCustom, calls=%fused_computation.clone.clone.1 | custom fusion | bytes 6291520 | tf_op jit(solution)/shard_map/while/body/eval_jaxpr/jit(_take)/gather | solution.py:28
  403.1 6.7 %select_add_fusion.4 = f32[16,3,128,128]{3,2,1,0:T(8,128)} fusion(f32[16,3,128,128]{3,2,1,0:T(8,128)} %get-tuple-element.149, f32[16,3,128,128]{3,2,1,0:T(8,128)} %gather_fusion, pred[16]{0:T(512)(128)(4,1)S(1)} %get-tuple-element.137, pred[]{:T(512)S(6)} %compare.18, f32[16,16,128,128]{3,2,1,0:T(8,128)} %get-tuple-element.162, s32[]{:T(128)} %get-tuple-element.148), kind=kOutput, calls=%fused_computation.5.clone.1 | convolution fusion | flops 1210318848 | bytes 10486289 | tf_op jit(solution)/shard_map/while/body/eval_jaxpr/akij,kjl->kail/dot_general | solution.py:45
  415.2 9.0 %convolution_bitcast_fusion = f32[16,128,128]{2,1,0:T(8,128)} fusion(f32[16,3,128,128]{3,2,1,0:T(8,128)} %get-tuple-element.41, f32[16,3,128,128]{3,2,1,0:T(8,128)} %get-tuple-element.40), kind=kOutput, calls=%fused_computation.24 | convolution fusion | flops 1207959552 | bytes 7340032 | tf_op jit(solution)/shard_map/kaij,kail->kjl/dot_general | solution.py:58
  428.4 120.4 %all-reduce.2.cloned.1.call-done = f32[16,128,128]{2,1,0:T(8,128)} async-done(((f32[16,128,128]{2,1,0:T(8,128)}), f32[16,128,128]{2,1,0:T(8,128)}) %all-reduce.2.cloned.1.call-update) | async-done | bytes 1048592 | tf_op jit(solution)/shard_map/psum | solution.py:63
  (187 shorter events, 124.5 us)
Async XLA Ops:
  7.2 1.2 copy-start
  7.2 82.3 %copy-start.1 = (f32[3,3,128,128]{3,2,1,0:T(8,128)S(1)}, f32[3,3,128,128]{3,2,1,0:T(8,128)}, u32[]{:S(2)}) copy-start(f32[3,3,128,128]{3,2,1,0:T(8,128)} %param.6) | copy-start | bytes 1769476
  7.2 119.1 %all-gather.2.cloned.1.call-start = ((), (), s32[]{:S(2)}) async-start(), calls=%async_computation | async-start | bytes 17825792 | tf_op jit(solution)/shard_map/all_gather | solution.py:53
  12.8 536.0 %all-reduce.2.cloned.1.call-start = ((), (), s32[]{:S(2)}) async-start(), calls=%async_computation.1 | async-start | bytes 2097152 | tf_op jit(solution)/shard_map/psum | solution.py:63
  12.9 17.1 %collective-permute-start = (f32[3,3,128,128]{3,2,1,0:T(8,128)}, f32[3,3,128,128]{3,2,1,0:T(8,128)S(1)}, u32[]{:S(2)}, u32[]{:S(2)}) collective-permute-start(f32[3,3,128,128]{3,2,1,0:T(8,128)} %param.6), channel_id=1, source_target_pairs={{0,1},{1,2},{2,3},{3,4},{4,5},{5,6},{6,7},{7,8},{8,9},{9,10},{10,1... | collective-permute-start | bytes 1769480 | tf_op jit(solution)/shard_map/ppermute | solution.py:17
  15.0 15.0 %collective-permute-start.1 = (f32[3,3,128,128]{3,2,1,0:T(8,128)}, f32[3,3,128,128]{3,2,1,0:T(8,128)S(1)}, u32[]{:S(2)}, u32[]{:S(2)}) collective-permute-start(f32[3,3,128,128]{3,2,1,0:T(8,128)} %param.6), channel_id=1, source_target_pairs={{0,15},{1,0},{2,1},{3,2},{4,3},{5,4},{6,5},{7,6},{8,7},{9,8},{10,9... | collective-permute-start | bytes 1769480 | tf_op jit(solution)/shard_map/ppermute | solution.py:20
  30.0 15.0 %copy-start.6 = (f32[3,3,128,128]{3,2,1,0:T(8,128)}, f32[3,3,128,128]{3,2,1,0:T(8,128)S(1)}, u32[]{:S(2)}) copy-start(f32[3,3,128,128]{3,2,1,0:T(8,128)S(1)} %collective-permute-done) | copy-start | bytes 1769476
  30.0 15.0 %collective-permute-start.2 = (f32[3,3,128,128]{3,2,1,0:T(8,128)S(1)}, f32[3,3,128,128]{3,2,1,0:T(8,128)S(1)}, u32[]{:S(2)}, u32[]{:S(2)}) collective-permute-start(f32[3,3,128,128]{3,2,1,0:T(8,128)S(1)} %collective-permute-done), channel_id=1, source_target_pairs={{0,1},{1,2},{2,3},{3,4},{4,5},{5,6},{6,7},{7,8},{8,9},{9,10},{10,1... | collective-permute-start | bytes 1769480 | tf_op jit(solution)/shard_map/ppermute | solution.py:17
  30.0 47.1 %copy-start.8 = (f32[3,3,128,128]{3,2,1,0:T(8,128)}, f32[3,3,128,128]{3,2,1,0:T(8,128)S(1)}, u32[]{:S(2)}) copy-start(f32[3,3,128,128]{3,2,1,0:T(8,128)S(1)} %collective-permute-done.1) | copy-start | bytes 1769476
  30.0 15.0 %collective-permute-start.3 = (f32[3,3,128,128]{3,2,1,0:T(8,128)S(1)}, f32[3,3,128,128]{3,2,1,0:T(8,128)S(1)}, u32[]{:S(2)}, u32[]{:S(2)}) collective-permute-start(f32[3,3,128,128]{3,2,1,0:T(8,128)S(1)} %collective-permute-done.1), channel_id=1, source_target_pairs={{0,15},{1,0},{2,1},{3,2},{4,3},{5,4},{6,5},{7,6},{8,7},{9,8},{10,9... | collective-permute-start | bytes 1769480 | tf_op jit(solution)/shard_map/ppermute | solution.py:20
  45.0 32.1 %copy-start.10 = (f32[3,3,128,128]{3,2,1,0:T(8,128)}, f32[3,3,128,128]{3,2,1,0:T(8,128)S(1)}, u32[]{:S(2)}) copy-start(f32[3,3,128,128]{3,2,1,0:T(8,128)S(1)} %collective-permute-done.2) | copy-start | bytes 1769476
  45.0 14.0 %collective-permute-start.4 = (f32[3,3,128,128]{3,2,1,0:T(8,128)S(1)}, f32[3,3,128,128]{3,2,1,0:T(8,128)S(1)}, u32[]{:S(2)}, u32[]{:S(2)}) collective-permute-start(f32[3,3,128,128]{3,2,1,0:T(8,128)S(1)} %collective-permute-done.2), channel_id=1, source_target_pairs={{0,1},{1,2},{2,3},{3,4},{4,5},{5,6},{6,7},{7,8},{8,9},{9,10},{10,1... | collective-permute-start | bytes 1769480 | tf_op jit(solution)/shard_map/ppermute | solution.py:17
  45.0 27.3 %copy-start.4 = (f32[3,3,128,128]{3,2,1,0:T(8,128)}, f32[3,3,128,128]{3,2,1,0:T(8,128)S(1)}, u32[]{:S(2)}) copy-start(f32[3,3,128,128]{3,2,1,0:T(8,128)S(1)} %collective-permute-done.3) | copy-start | bytes 1769476
  45.0 14.0 %collective-permute-start.5 = (f32[3,3,128,128]{3,2,1,0:T(8,128)S(1)}, f32[3,3,128,128]{3,2,1,0:T(8,128)S(1)}, u32[]{:S(2)}, u32[]{:S(2)}) collective-permute-start(f32[3,3,128,128]{3,2,1,0:T(8,128)S(1)} %collective-permute-done.3), channel_id=1, source_target_pairs={{0,15},{1,0},{2,1},{3,2},{4,3},{5,4},{6,5},{7,6},{8,7},{9,8},{10,9... | collective-permute-start | bytes 1769480 | tf_op jit(solution)/shard_map/ppermute | solution.py:20
  59.0 13.2 %collective-permute-start.6 = (f32[3,3,128,128]{3,2,1,0:T(8,128)S(1)}, f32[3,3,128,128]{3,2,1,0:T(8,128)}, u32[]{:S(2)}, u32[]{:S(2)}) collective-permute-start(f32[3,3,128,128]{3,2,1,0:T(8,128)S(1)} %collective-permute-done.4), channel_id=1, source_target_pairs={{0,1},{1,2},{2,3},{3,4},{4,5},{5,6},{6,7},{7,8},{8,9},{9,10},{10,1... | collective-permute-start | bytes 1769480 | tf_op jit(solution)/shard_map/ppermute | solution.py:17
  59.0 13.2 %copy-start.2 = (f32[3,3,128,128]{3,2,1,0:T(8,128)}, f32[3,3,128,128]{3,2,1,0:T(8,128)S(1)}, u32[]{:S(2)}) copy-start(f32[3,3,128,128]{3,2,1,0:T(8,128)S(1)} %collective-permute-done.5) | copy-start | bytes 1769476
  59.0 13.2 %collective-permute-start.7 = (f32[3,3,128,128]{3,2,1,0:T(8,128)S(1)}, f32[3,3,128,128]{3,2,1,0:T(8,128)}, u32[]{:S(2)}, u32[]{:S(2)}) collective-permute-start(f32[3,3,128,128]{3,2,1,0:T(8,128)S(1)} %collective-permute-done.5), channel_id=1, source_target_pairs={{0,15},{1,0},{2,1},{3,2},{4,3},{5,4},{6,5},{7,6},{8,7},{9,8},{10,9... | collective-permute-start | bytes 1769480 | tf_op jit(solution)/shard_map/ppermute | solution.py:20
  72.3 12.4 %collective-permute-start.8 = (f32[3,3,128,128]{3,2,1,0:T(8,128)}, f32[3,3,128,128]{3,2,1,0:T(8,128)}, u32[]{:S(2)}, u32[]{:S(2)}) collective-permute-start(f32[3,3,128,128]{3,2,1,0:T(8,128)} %collective-permute-done.6), channel_id=1, source_target_pairs={{0,1},{1,2},{2,3},{3,4},{4,5},{5,6},{6,7},{7,8},{8,9},{9,10},{10,1... | collective-permute-start | bytes 1769480 | tf_op jit(solution)/shard_map/ppermute | solution.py:17
  72.3 20.7 %collective-permute-start.9 = (f32[3,3,128,128]{3,2,1,0:T(8,128)}, f32[3,3,128,128]{3,2,1,0:T(8,128)S(1)}, u32[]{:S(2)}, u32[]{:S(2)}) collective-permute-start(f32[3,3,128,128]{3,2,1,0:T(8,128)} %collective-permute-done.7), channel_id=1, source_target_pairs={{0,15},{1,0},{2,1},{3,2},{4,3},{5,4},{6,5},{7,6},{8,7},{9,8},{10,9... | collective-permute-start | bytes 1769480 | tf_op jit(solution)/shard_map/ppermute | solution.py:20
  77.9 12.5 %copy-start.7 = (f32[3,3,128,128]{3,2,1,0:T(8,128)S(1)}, f32[3,3,128,128]{3,2,1,0:T(8,128)}, u32[]{:S(2)}) copy-start(f32[3,3,128,128]{3,2,1,0:T(8,128)} %copy-done.6) | copy-start | bytes 1769476
  77.9 13.3 %copy-start.9 = (f32[3,3,128,128]{3,2,1,0:T(8,128)S(1)}, f32[3,3,128,128]{3,2,1,0:T(8,128)}, u32[]{:S(2)}) copy-start(f32[3,3,128,128]{3,2,1,0:T(8,128)} %copy-done.8) | copy-start | bytes 1769476
  77.9 14.2 %copy-start.11 = (f32[3,3,128,128]{3,2,1,0:T(8,128)S(1)}, f32[3,3,128,128]{3,2,1,0:T(8,128)}, u32[]{:S(2)}) copy-start(f32[3,3,128,128]{3,2,1,0:T(8,128)} %copy-done.10) | copy-start | bytes 1769476
  77.9 19.8 %copy-start.5 = (f32[3,3,128,128]{3,2,1,0:T(8,128)S(1)}, f32[3,3,128,128]{3,2,1,0:T(8,128)}, u32[]{:S(2)}) copy-start(f32[3,3,128,128]{3,2,1,0:T(8,128)} %copy-done.4) | copy-start | bytes 1769476
  77.9 21.5 %copy-start.3 = (f32[3,3,128,128]{3,2,1,0:T(8,128)S(1)}, f32[3,3,128,128]{3,2,1,0:T(8,128)}, u32[]{:S(2)}) copy-start(f32[3,3,128,128]{3,2,1,0:T(8,128)} %copy-done.2) | copy-start | bytes 1769476
  84.6 14.0 %collective-permute-start.10 = (f32[3,3,128,128]{3,2,1,0:T(8,128)}, f32[3,3,128,128]{3,2,1,0:T(8,128)S(1)}, u32[]{:S(2)}, u32[]{:S(2)}) collective-permute-start(f32[3,3,128,128]{3,2,1,0:T(8,128)} %collective-permute-done.8), channel_id=1, source_target_pairs={{0,1},{1,2},{2,3},{3,4},{4,5},{5,6},{6,7},{7,8},{8,9},{9,10},{10,1... | collective-permute-start | bytes 1769480 | tf_op jit(solution)/shard_map/ppermute | solution.py:17
  92.9 11.6 %collective-permute-start.11 = (f32[3,3,128,128]{3,2,1,0:T(8,128)S(1)}, f32[3,3,128,128]{3,2,1,0:T(8,128)S(1)}, u32[]{:S(2)}, u32[]{:S(2)}) collective-permute-start(f32[3,3,128,128]{3,2,1,0:T(8,128)S(1)} %collective-permute-done.9), channel_id=1, source_target_pairs={{0,15},{1,0},{2,1},{3,2},{4,3},{5,4},{6,5},{7,6},{8,7},{9,8},{10,9... | collective-permute-start | bytes 1769480 | tf_op jit(solution)/shard_map/ppermute | solution.py:20
  98.6 13.1 %collective-permute-start.12 = (f32[3,3,128,128]{3,2,1,0:T(8,128)S(1)}, f32[3,3,128,128]{3,2,1,0:T(8,128)S(1)}, u32[]{:S(2)}, u32[]{:S(2)}) collective-permute-start(f32[3,3,128,128]{3,2,1,0:T(8,128)S(1)} %collective-permute-done.10), channel_id=1, source_target_pairs={{0,1},{1,2},{2,3},{3,4},{4,5},{5,6},{6,7},{7,8},{8,9},{9,10},{10,1... | collective-permute-start | bytes 1769480 | tf_op jit(solution)/shard_map/ppermute | solution.py:17
  104.6 14.4 %collective-permute-start.13 = (f32[3,3,128,128]{3,2,1,0:T(8,128)S(1)}, f32[3,3,128,128]{3,2,1,0:T(8,128)S(1)}, u32[]{:S(2)}, u32[]{:S(2)}) collective-permute-start(f32[3,3,128,128]{3,2,1,0:T(8,128)S(1)} %collective-permute-done.11), channel_id=1, source_target_pairs={{0,15},{1,0},{2,1},{3,2},{4,3},{5,4},{6,5},{7,6},{8,7},{9,8},{10,9... | collective-permute-start | bytes 1769480 | tf_op jit(solution)/shard_map/ppermute | solution.py:20
  111.8 13.6 %collective-permute-start.14 = (f32[3,3,128,128]{3,2,1,0:T(8,128)S(1)}, f32[3,3,128,128]{3,2,1,0:T(8,128)S(1)}, u32[]{:S(2)}, u32[]{:S(2)}) collective-permute-start(f32[3,3,128,128]{3,2,1,0:T(8,128)S(1)} %collective-permute-done.12), channel_id=1, source_target_pairs={{0,1},{1,2},{2,3},{3,4},{4,5},{5,6},{6,7},{7,8},{8,9},{9,10},{10,1... | collective-permute-start | bytes 1769480 | tf_op jit(solution)/shard_map/ppermute | solution.py:17
  126.3 297.9 %copy-start.12 = (s32[16,16]{1,0:T(8,128)S(1)}, s32[16,16]{1,0:T(8,128)}, u32[]{:S(2)}) copy-start(s32[16,16]{1,0:T(8,128)} %param.9) | copy-start | bytes 3076
Sparse Core Ops, SparseCore 0:
  12.9 99.6 all-gather.1
  424.3 124.4 all-reduce.1
